TPU v7x, 512 devices: a whole 4x4x16 slice. The times are simulated.
512 devices in a mesh: blk: 128 (over y, z_lo, x, core), head: 4 (over z_hi).
Axes of the slice: x: 4, y: 4, z: 16 (z_hi: 4, z_lo: 4; z = z_hi * 4 + z_lo), core: 2. Of those that a mesh axis runs over, the one named last changes fastest.
Arguments:
- query_states: bfloat16 [128, 2, 64, 2048], P('blk', None, 'head'), may hold values from -24 to 24
- key_states: bfloat16 [128, 2, 64, 512], P('blk', None, None, 'head'), may hold values from -6 to 6
- value_states: bfloat16 [128, 2, 64, 512], P('blk', None, None, 'head'), may hold values from -6 to 6
- doc_lengths: int32 [3], replicated, may hold values from 1 to 12288, 16384 in all
- page_slot: int32 [128, 2, 4], replicated, may hold values from 0 to 2047, as said below
Outputs:
- attended: bfloat16 [128, 2, 64, 2048], P('blk', None, None, 'head')
- kv_cache: bfloat16 [2048, 4, 16, 256], P('blk', 'head')
Inputs may be any that keep to these rules, and one draw needn't show every extreme that they name: `page_slot`: all entries differ. The busiest owners hold 16 pages, the least busy 4.
All inputs are finite; a program needn't handle non-finite values.
Results may differ from a plain program's by a relative error of at most 0.007.
Values may be sent and summed in bfloat16 or wider, within the bound.
A program may use at most 64 MiB of HBM per device.

v0:
```python
import jax
import jax.numpy as jnp
from jax import lax
from jax.sharding import PartitionSpec as P

PAGE = 16


def per_device(query_states, key_states, value_states, doc_lengths, page_slot):
    q_local = lax.all_to_all(query_states, "head", split_axis=3, concat_axis=2, tiled=True)
    axis_count = lax.axis_size("blk")
    my_index = lax.axis_index("blk")
    block_tok = q_local.shape[2]
    head_dim = key_states.shape[3]
    group_size = q_local.shape[3] // head_dim
    query_rows = q_local.reshape(2 * block_tok, group_size, head_dim)
    offsets = jnp.arange(block_tok, dtype=jnp.int32)
    doc_bounds = jnp.cumsum(doc_lengths)[:-1]
    page_count = block_tok // PAGE
    slot_count = 4 * page_count
    slot_range = jnp.arange(slot_count, dtype=jnp.int32)
    score_scale = head_dim ** (-0.5)

    def group_positions(owner_ids):
        block_starts = jnp.stack([owner_ids, 2 * axis_count - 1 - owner_ids], axis=1) * block_tok
        return (block_starts[:, :, None] + offsets[None, None, :]).reshape(-1)

    def doc_of(positions):
        return jnp.sum((positions[:, None] >= doc_bounds[None, :]).astype(jnp.int32), axis=1)

    q_pos = group_positions(my_index.reshape(1))
    q_doc = doc_of(q_pos)

    def attend_group(attn_state, key_rows, value_rows, allowed):
        running_max, weight_sum, accum = attn_state
        scores = (
            jnp.einsum("qhd,kd->qhk", query_rows, key_rows, preferred_element_type=jnp.float32)
            * score_scale
        )
        masked = jnp.where(allowed[:, None, :], scores, -1e30)
        new_max = jnp.maximum(running_max, jnp.max(masked, axis=2))
        weights = jnp.where(allowed[:, None, :], jnp.exp(masked - new_max[..., None]), 0.0)
        factor = jnp.exp(running_max - new_max)
        weight_sum = weight_sum * factor + jnp.sum(weights, axis=2)
        update = jnp.einsum(
            "qhk,kd->qhd",
            weights.astype(jnp.bfloat16),
            value_rows,
            preferred_element_type=jnp.float32,
        )
        accum = accum * factor[..., None] + update
        return (new_max, weight_sum, accum)

    def visit_group(attn_state, key_group, value_group, owner_ids):
        key_rows = key_group.reshape(-1, head_dim)
        value_rows = value_group.reshape(-1, head_dim)
        k_pos = group_positions(owner_ids)
        allowed = (k_pos[None, :] <= q_pos[:, None]) & (doc_of(k_pos)[None, :] == q_doc[:, None])
        return attend_group(attn_state, key_rows, value_rows, allowed)

    def place_pages(page_store, key_group, value_group, owner_ids):
        page_rows = jnp.concatenate([key_group, value_group], axis=-1).reshape(
            -1, PAGE * 2 * head_dim
        )
        slot_ids = jnp.take(page_slot, owner_ids, axis=0).reshape(-1) - my_index * slot_count
        selector = (slot_range[:, None] == slot_ids[None, :]).astype(jnp.bfloat16)
        return page_store + jnp.dot(selector, page_rows, preferred_element_type=jnp.float32)

    def fold_groups(step_fn, carried, kv_piece):
        key_piece, value_piece = kv_piece
        piece_len = key_piece.shape[0]
        width = 4
        owner_ids = jnp.arange(piece_len, dtype=jnp.int32).reshape(piece_len // width, width)
        key_groups = key_piece.reshape(piece_len // width, width, 2, block_tok, head_dim)
        value_groups = value_piece.reshape(piece_len // width, width, 2, block_tok, head_dim)

        def visit_one(inner_state, entry_tuple):
            key_group, value_group, owners = entry_tuple
            return (step_fn(inner_state, key_group, value_group, owners), None)

        return lax.scan(visit_one, carried, (key_groups, value_groups, owner_ids))[0]

    empty_store = jnp.zeros((slot_count, PAGE * 2 * head_dim), jnp.float32)
    start_state = (
        jnp.full((2 * block_tok, group_size), -1e30, jnp.float32),
        jnp.zeros((2 * block_tok, group_size), jnp.float32),
        jnp.zeros((2 * block_tok, group_size, head_dim), jnp.float32),
    )
    final_state = fold_groups(
        visit_group,
        start_state,
        (
            lax.all_gather(key_states, "blk", axis=0, tiled=True),
            lax.all_gather(value_states, "blk", axis=0, tiled=True),
        ),
    )
    page_store = fold_groups(
        place_pages,
        empty_store,
        (
            lax.all_gather(key_states, "blk", axis=0, tiled=True),
            lax.all_gather(value_states, "blk", axis=0, tiled=True),
        ),
    )
    running_max, weight_sum, accum = final_state
    attended = (
        (accum / weight_sum[..., None])
        .astype(jnp.bfloat16)
        .reshape(1, 2, block_tok, group_size * head_dim)
    )
    kv_cache = page_store.astype(jnp.bfloat16).reshape(slot_count, 1, PAGE, 2 * head_dim)
    return (attended, kv_cache)


def solution(mesh):
    return jax.shard_map(
        per_device,
        mesh=mesh,
        in_specs=(
            P("blk", None, "head", None),
            P("blk", None, None, "head"),
            P("blk", None, None, "head"),
            P(),
            P(),
        ),
        out_specs=(P("blk", None, None, "head"), P("blk", "head", None, None)),
        check_vma=False,
    )
```

profile of v0, /device:TPU:1, one launch (start us, length us, event | category | flops | bytes accessed | tf_op | source)
XLA Modules:
  0.0 593.8 jit_solution(2853987302329961732)
XLA Ops:
  8.6 2.0 copy.26
  10.7 1.7 reshape.326
  12.4 15.6 %all-to-all-start = ((bf16[4,2,8192]{2,1,0:T(2,128)(2,1)}), bf16[4,2,8192]{2,1,0:T(2,128)(2,1)S(1)}, u32[]{:S(2)}, u32[]{:S(2)}) async-start(bf16[4,2,8192]{2,1,0:T(2,128)(2,1)} %reshape.326), calls=%async_computation | async-start | bytes 262144 | tf_op jit(solution)/shard_map/all_to_all | solution.py:10
  30.2 10.6 %all-to-all-done = bf16[4,2,8192]{2,1,0:T(2,128)(2,1)S(1)} async-done(((bf16[4,2,8192]{2,1,0:T(2,128)(2,1)}), bf16[4,2,8192]{2,1,0:T(2,128)(2,1)S(1)}, u32[]{:S(2)}, u32[]{:S(2)}) %all-to-all-start) | async-done | bytes 131104 | tf_op jit(solution)/shard_map/all_to_all | solution.py:10
  42.1 178.9 %all-gather.3.cloned.1.call-done = bf16[128,2,64,128]{3,2,1,0:T(8,128)(2,1)} async-done(((bf16[1,2,64,128]{3,2,1,0:T(8,128)(2,1)}), bf16[128,2,64,128]{3,2,1,0:T(8,128)(2,1)}) %all-gather.3.cloned.1.call-update) | async-done | bytes 4194320 | tf_op jit(solution)/shard_map/all_gather | solution.py:93
  221.1 205.9 %all-gather.5.cloned.1.call-done = bf16[128,2,64,128]{3,2,1,0:T(8,128)(2,1)} async-done(((bf16[1,2,64,128]{3,2,1,0:T(8,128)(2,1)}), bf16[128,2,64,128]{3,2,1,0:T(8,128)(2,1)}) %all-gather.5.cloned.1.call-update) | async-done | bytes 4194320 | tf_op jit(solution)/shard_map/all_gather | solution.py:94
  427.0 88.9 %while.28 = (s32[]{:T(128)}, f32[128,4]{0,1:T(4,128)S(1)}, f32[128,4]{0,1:T(4,128)S(1)}, f32[128,4,128]{2,0,1:T(8,128)S(1)}, s32[32,4]{1,0:T(8,128)S(1)}, /*inde...) while((s32[]{:T(128)}, f32[128,4]{0,1:T(4,128)S(1)}, ...), condition=%wide.region_6.7_spmd.clone, body=%wide.region_2.6_spmd.clone.sunk | while | flops 136976032 | bytes 4899697 | solution.py:81
  427.8 1.0 constant_dynamic-slice_fusion.5
  430.5 1.0 constant_dynamic-slice_fusion.5
  433.3 1.0 constant_dynamic-slice_fusion.5
  436.1 1.0 constant_dynamic-slice_fusion.5
  438.9 1.0 constant_dynamic-slice_fusion.5
  441.7 1.0 constant_dynamic-slice_fusion.5
  444.4 1.0 constant_dynamic-slice_fusion.5
  447.2 1.0 constant_dynamic-slice_fusion.5
  450.0 1.0 constant_dynamic-slice_fusion.5
  455.6 1.0 constant_dynamic-slice_fusion.5
  458.3 1.0 constant_dynamic-slice_fusion.5
  461.1 1.0 constant_dynamic-slice_fusion.5
  463.9 1.0 constant_dynamic-slice_fusion.5
  466.7 1.0 constant_dynamic-slice_fusion.5
  469.4 1.0 constant_dynamic-slice_fusion.5
  472.2 1.0 constant_dynamic-slice_fusion.5
  477.8 1.0 constant_dynamic-slice_fusion.5
  480.6 1.0 constant_dynamic-slice_fusion.5
  483.3 1.0 constant_dynamic-slice_fusion.5
  486.1 1.0 constant_dynamic-slice_fusion.5
  488.9 1.0 constant_dynamic-slice_fusion.5
  491.7 1.0 constant_dynamic-slice_fusion.5
  494.5 1.0 constant_dynamic-slice_fusion.5
  497.2 1.0 constant_dynamic-slice_fusion.5
  516.9 69.3 %while.29 = (s32[]{:T(128)}, f32[16,4096]{1,0:T(8,128)S(1)}, s32[32,4]{1,0:T(8,128)S(1)}, s32[128,2,4]{2,1,0:T(2,128)S(1)}, s32[]{:T(128)}, /*index=5*/bf16[32,4...) while((s32[]{:T(128)}, f32[16,4096]{1,0:T(8,128)S(1)}, ...), condition=%wide.region_8.9_spmd.clone, body=%wide.region_7.8_spmd.clone.sunk | while | flops 4851303 | bytes 2364495 | solution.py:81
  (836 shorter events, 136.5 us)
Async XLA Ops:
  7.2 213.9 %all-gather.3.cloned.1.call-start = ((), (), s32[]{:S(2)}) async-start(), calls=%async_computation.1 | async-start | bytes 4227072 | tf_op jit(solution)/shard_map/all_gather | solution.py:93
  7.9 419.1 %all-gather.5.cloned.1.call-start = ((), (), s32[]{:S(2)}) async-start(), calls=%async_computation.2 | async-start | bytes 4227072 | tf_op jit(solution)/shard_map/all_gather | solution.py:94
  12.4 28.3 %all-to-all-start = ((bf16[4,2,8192]{2,1,0:T(2,128)(2,1)}), bf16[4,2,8192]{2,1,0:T(2,128)(2,1)S(1)}, u32[]{:S(2)}, u32[]{:S(2)}) async-start(bf16[4,2,8192]{2,1,0:T(2,128)(2,1)} %reshape.326), calls=%async_computation | async-start | bytes 262144 | tf_op jit(solution)/shard_map/all_to_all | solution.py:10
Sparse Core Ops, SparseCore 0:
  10.2 210.8 all-gather.2
  223.2 203.7 all-gather.4
where the time goes:
time: 595 us; the launch traced here: 594 us
  waiting for transfers between devices  397 us (67%)
  local copies, waits for them, and re-layouts  105 us (18%)
  matrix products  30.2 us (5%)
  other arithmetic  27.7 us (5%)
  starting transfers between devices  15.7 us (3%)
  between operations  14.1 us (2%)
    all_gather x1, waiting for transfers between devices, per_device(): lax.all_gather(value_states, 'blk', axis=0, tiled=True)  206 us
    all_gather x1, waiting for transfers between devices, per_device(): lax.all_gather(key_states, 'blk', axis=0, tiled=True)  179 us
    dynamic_slice x32, local copies, waits for them, and re-layouts, fold_groups(): lax.scan(visit_one, carried, (key_groups, value_groups, owner_ids))[0]  31.8 us
    squeeze x32, local copies, waits for them, and re-layouts, fold_groups(): lax.scan(visit_one, carried, (key_groups, value_groups, owner_ids))[0]  31.7 us
    gather x32, local copies, waits for them, and re-layouts, place_pages(): jnp.take(page_slot, owner_ids, axis=0).reshape(-1) - my_index * slot_count  18.3 us
    all_to_all x1, starting transfers between devices, per_device(): lax.all_to_all(query_states, 'head', split_axis=3, concat_axis=2, tiled=T...  15.6 us
    dot_general x32, matrix products, attend_group(): jnp.einsum('qhk,kd->qhd', weights.astype(jnp.bfloat16), value_rows, prefe...  14.1 us
  transfers between devices with their start and end apart: 3, of which 3 were waited for; matrix products, arithmetic and copies ran while one was open for 1% of the time, Pallas kernels for 0%

commit v1 on v0

--- a/solution.py
+++ b/solution.py
@@ -2,6 +2,7 @@
 import jax.numpy as jnp
 from jax import lax
 from jax.sharding import PartitionSpec as P
+from jax.lax import all_to_all, axis_size
 
 PAGE = 16
 
@@ -86,13 +87,19 @@
         jnp.zeros((2 * block_tok, group_size), jnp.float32),
         jnp.zeros((2 * block_tok, group_size, head_dim), jnp.float32),
     )
+
+    def _map_table(mat, lane_axis):
+        copies = []
+        for _ in range(axis_size(lane_axis)):
+            copies.append(mat)
+        h_now = jnp.stack(copies, 0)
+        top = all_to_all(h_now, axis_name=lane_axis, split_axis=0, concat_axis=0)
+        return jnp.concatenate(top, 0)
+
     final_state = fold_groups(
         visit_group,
         start_state,
-        (
-            lax.all_gather(key_states, "blk", axis=0, tiled=True),
-            lax.all_gather(value_states, "blk", axis=0, tiled=True),
-        ),
+        (lax.all_gather(key_states, "blk", axis=0, tiled=True), _map_table(value_states, "blk")),
     )
     page_store = fold_groups(
         place_pages,

time: 595 us -> 620 us (1.042)
  starting transfers between devices: 15.7 us -> 28.5 us
  waiting for transfers between devices: 397 us -> 405 us
    all_to_all x0 -> x1, starting transfers between devices: none -> 12.8 us  [_map_table(): top = all_to_all(h_now, axis_name=lane_axis, split_axis=0, concat_axis=0)]
    all_gather x1, waiting for transfers between devices: 179 us -> 186 us  [per_device(): lax.all_gather(key_states, 'blk', axis=0, tiled=True)]
  transfers between devices with their start and end apart: 3 -> 4, of which waited for: 3 -> 3; matrix products, arithmetic and copies ran while one was open for 1% -> 13% of each run, Pallas kernels for 0% -> 0%
where the time goes in v1:
time: 620 us; the launch traced here: 618 us
  waiting for transfers between devices  405 us (65%)
  local copies, waits for them, and re-layouts  108 us (17%)
  matrix products  30.5 us (5%)
  starting transfers between devices  28.5 us (5%)
  other arithmetic  27.7 us (4%)
  between operations  14.2 us (2%)
    all_gather x1, waiting for transfers between devices, per_device(): lax.all_gather(value_states, 'blk', axis=0, tiled=True)  206 us
    all_gather x1, waiting for transfers between devices, per_device(): lax.all_gather(key_states, 'blk', axis=0, tiled=True)  186 us
    dynamic_slice x32, local copies, waits for them, and re-layouts, fold_groups(): lax.scan(visit_one, carried, (key_groups, value_groups, owner_ids))[0]  31.8 us
    squeeze x32, local copies, waits for them, and re-layouts, fold_groups(): lax.scan(visit_one, carried, (key_groups, value_groups, owner_ids))[0]  31.7 us
    gather x32, local copies, waits for them, and re-layouts, place_pages(): jnp.take(page_slot, owner_ids, axis=0).reshape(-1) - my_index * slot_count  18.3 us
    all_to_all x1, starting transfers between devices, per_device(): lax.all_to_all(query_states, 'head', split_axis=3, concat_axis=2, tiled=T...  15.6 us
    dot_general x32, matrix products, attend_group(): jnp.einsum('qhk,kd->qhd', weights.astype(jnp.bfloat16), value_rows, prefe...  14.5 us
    all_to_all x1, starting transfers between devices, _map_table(): top = all_to_all(h_now, axis_name=lane_axis, split_axis=0, concat_axis=0)  12.8 us
  transfers between devices with their start and end apart: 4, of which 3 were waited for; matrix products, arithmetic and copies ran while one was open for 13% of the time, Pallas kernels for 0%

profile of v1, /device:TPU:1, one launch (start us, length us, event | category | flops | bytes accessed | tf_op | source)
XLA Modules:
  0.0 618.4 jit_solution(6852762639450905380)
XLA Ops:
  8.6 2.0 copy.26
  10.7 1.7 reshape.328
  12.4 15.6 %all-to-all-start = ((bf16[4,2,8192]{2,1,0:T(2,128)(2,1)}), bf16[4,2,8192]{2,1,0:T(2,128)(2,1)S(1)}, u32[]{:S(2)}, u32[]{:S(2)}) async-start(bf16[4,2,8192]{2,1,0:T(2,128)(2,1)} %reshape.328), calls=%async_computation | async-start | bytes 262144 | tf_op jit(solution)/shard_map/all_to_all | solution.py:11
  30.2 10.6 %all-to-all-done = bf16[4,2,8192]{2,1,0:T(2,128)(2,1)S(1)} async-done(((bf16[4,2,8192]{2,1,0:T(2,128)(2,1)}), bf16[4,2,8192]{2,1,0:T(2,128)(2,1)S(1)}, u32[]{:S(2)}, u32[]{:S(2)}) %all-to-all-start) | async-done | bytes 131104 | tf_op jit(solution)/shard_map/all_to_all | solution.py:11
  40.7 3.8 stack.12
  44.5 12.8 %all-to-all-start.1 = ((bf16[128,1,2,64,128]{4,3,2,1,0:T(8,128)(2,1)}), bf16[128,1,2,64,128]{4,3,2,1,0:T(8,128)(2,1)}, u32[]{:S(2)}, u32[]{:S(2)}) async-start(bf16[128,1,2,64,128]{4,3,2,1,0:T(8,128)(2,1)} %stack.12), calls=%async_computation.1 | async-start | bytes 8388608 | tf_op jit(solution)/shard_map/all_to_all | solution.py:96
  58.7 186.4 %all-gather.3.cloned.1.call-done = bf16[128,2,64,128]{3,2,1,0:T(8,128)(2,1)} async-done(((bf16[1,2,64,128]{3,2,1,0:T(8,128)(2,1)}), bf16[128,2,64,128]{3,2,1,0:T(8,128)(2,1)}) %all-gather.3.cloned.1.call-update) | async-done | bytes 4194320 | tf_op jit(solution)/shard_map/all_gather | solution.py:102
  245.1 206.2 %all-gather.5.cloned.1.call-done = bf16[128,2,64,128]{3,2,1,0:T(8,128)(2,1)} async-done(((bf16[1,2,64,128]{3,2,1,0:T(8,128)(2,1)}), bf16[128,2,64,128]{3,2,1,0:T(8,128)(2,1)}) %all-gather.5.cloned.1.call-update) | async-done | bytes 4194320 | tf_op jit(solution)/shard_map/all_gather | solution.py:109
  451.4 69.3 %while.29 = (s32[]{:T(128)}, f32[16,4096]{1,0:T(8,128)S(1)}, s32[32,4]{1,0:T(8,128)S(1)}, s32[128,2,4]{2,1,0:T(2,128)S(1)}, s32[]{:T(128)}, /*index=5*/bf16[32,4...) while((s32[]{:T(128)}, f32[16,4096]{1,0:T(8,128)S(1)}, ...), condition=%wide.region_8.9_spmd.clone, body=%wide.region_7.8_spmd.clone.sunk | while | flops 4851303 | bytes 2364495 | solution.py:82
  521.4 89.2 %while.28 = (s32[]{:T(128)}, f32[128,4]{0,1:T(4,128)S(1)}, f32[128,4]{0,1:T(4,128)S(1)}, f32[128,4,128]{2,0,1:T(8,128)S(1)}, s32[32,4]{1,0:T(8,128)S(1)}, /*inde...) while((s32[]{:T(128)}, f32[128,4]{0,1:T(4,128)S(1)}, ...), condition=%wide.region_6.7_spmd.clone, body=%wide.region_2.6_spmd.clone.sunk | while | flops 136976032 | bytes 4899697 | solution.py:82
  522.1 1.0 constant_dynamic-slice_fusion.5
  524.9 1.0 constant_dynamic-slice_fusion.5
  527.7 1.0 constant_dynamic-slice_fusion.5
  530.5 1.0 constant_dynamic-slice_fusion.5
  533.3 1.0 constant_dynamic-slice_fusion.5
  538.8 1.0 constant_dynamic-slice_fusion.5
  541.6 1.0 constant_dynamic-slice_fusion.5
  544.4 1.0 constant_dynamic-slice_fusion.5
  547.2 1.0 constant_dynamic-slice_fusion.5
  550.0 1.0 constant_dynamic-slice_fusion.5
  552.8 1.0 constant_dynamic-slice_fusion.5
  558.3 1.0 constant_dynamic-slice_fusion.5
  561.1 1.0 constant_dynamic-slice_fusion.5
  563.9 1.0 constant_dynamic-slice_fusion.5
  566.7 1.0 constant_dynamic-slice_fusion.5
  569.5 1.0 constant_dynamic-slice_fusion.5
  572.3 1.0 constant_dynamic-slice_fusion.5
  575.1 1.0 constant_dynamic-slice_fusion.5
  577.9 1.0 constant_dynamic-slice_fusion.5
  580.6 1.0 constant_dynamic-slice_fusion.5
  583.4 1.0 constant_dynamic-slice_fusion.5
  586.2 1.0 constant_dynamic-slice_fusion.5
  (839 shorter events, 138.7 us)
Async XLA Ops:
  7.2 238.0 %all-gather.3.cloned.1.call-start = ((), (), s32[]{:S(2)}) async-start(), calls=%async_computation.2 | async-start | bytes 4227072 | tf_op jit(solution)/shard_map/all_gather | solution.py:102
  7.9 443.5 %all-gather.5.cloned.1.call-start = ((), (), s32[]{:S(2)}) async-start(), calls=%async_computation.3 | async-start | bytes 4227072 | tf_op jit(solution)/shard_map/all_gather | solution.py:109
  12.4 28.3 %all-to-all-start = ((bf16[4,2,8192]{2,1,0:T(2,128)(2,1)}), bf16[4,2,8192]{2,1,0:T(2,128)(2,1)S(1)}, u32[]{:S(2)}, u32[]{:S(2)}) async-start(bf16[4,2,8192]{2,1,0:T(2,128)(2,1)} %reshape.328), calls=%async_computation | async-start | bytes 262144 | tf_op jit(solution)/shard_map/all_to_all | solution.py:11
  44.5 476.9 %all-to-all-start.1 = ((bf16[128,1,2,64,128]{4,3,2,1,0:T(8,128)(2,1)}), bf16[128,1,2,64,128]{4,3,2,1,0:T(8,128)(2,1)}, u32[]{:S(2)}, u32[]{:S(2)}) async-start(bf16[128,1,2,64,128]{4,3,2,1,0:T(8,128)(2,1)} %stack.12), calls=%async_computation.1 | async-start | bytes 8388608 | tf_op jit(solution)/shard_map/all_to_all | solution.py:96
Sparse Core Ops, SparseCore 0:
  10.2 234.9 all-gather.2
  247.3 204.0 all-gather.4
